TPU v7x, 256 devices: a whole 4x4x8 slice. The times are simulated.
256 devices in a mesh: row: 16 (over y, x), col: 16 (over z, core).
Axes of the slice: x: 4, y: 4, z: 8, core: 2. Of those that a mesh axis runs over, the one named last changes fastest.
Arguments:
- block_values: float32 [16, 16, 40, 128, 128], P('row', 'col'), may hold values from 7.8125e-06 to 0.00078125
- block_index: int32 [16, 16, 2, 40], P('row', 'col'), may hold values from 0 to 31, as said below
- block_count: int32 [16, 16], P('row', 'col'), may hold values from 1 to 40, as said below
- strength: float32 [32], replicated, may hold values from 1 to 30
- raw_scores: float32 [512, 32, 128], P(('row', 'col')), may hold values from -24 to 24
Outputs:
- smoothed: float32 [512, 32, 128], P(('row', 'col'))
- final_residual: float32 [512, 32, 128], P(('row', 'col'))
Inputs may be any that keep to these rules, and one draw needn't show every extreme that they name: `block_count`: some device has exactly 40 live slots; the others hold between half and all of their share of the upper triangle, scaled to 40. `block_index`: the live slots of one device name distinct blocks, each with global block row at most its global block column; slots at or above the count hold pairs in range that are ignored.
All inputs are finite; a program needn't handle non-finite values.
Results may differ from a plain program's by a relative error of at most 0.0003.
Values sent between devices are 32-bit elements; how exact they have to be, the bound alone decides.
A program may use at most 64 MiB of HBM per device.

v0:
```python
import jax
import jax.numpy as jnp
from jax import lax
from jax.sharding import PartitionSpec as P

ITERS = 3


def local_terms(values, row_index, col_index, panel_rows, panel_cols):
    picked_cols = jnp.take(panel_cols, col_index, axis=0)
    picked_rows = jnp.take(panel_rows, row_index, axis=0)
    to_rows = jnp.einsum("crk,cik->cri", picked_cols, values, precision=lax.Precision.HIGHEST)
    to_cols = jnp.einsum("cri,cik->crk", picked_rows, values, precision=lax.Precision.HIGHEST)
    row_part = jax.ops.segment_sum(to_rows, row_index, num_segments=panel_rows.shape[0])
    col_part = jax.ops.segment_sum(to_cols, col_index, num_segments=panel_cols.shape[0])
    return (row_part, col_part)


def fold_terms(row_part, col_part):
    return lax.psum_scatter(row_part, "col", scatter_dimension=0, tiled=True) + lax.psum_scatter(
        col_part, "row", scatter_dimension=0, tiled=True
    )


def total(field):
    return jnp.sum(field, axis=(0, 2))


def global_sum(partial_sum):
    return lax.psum(partial_sum, ("row", "col"))


def shards(block_values, block_index, block_count, strength, raw_scores):
    values = block_values[0, 0]
    row_index = block_index[0, 0, 0]
    col_index = block_index[0, 0, 1]
    live_mask = (jnp.arange(values.shape[0], dtype=jnp.int32) < block_count[0, 0]).astype(
        jnp.float32
    )
    masked = values * live_mask[:, None, None]
    segment = raw_scores.shape[0]
    block_size = raw_scores.shape[2]
    rows_here = lax.axis_size("col") * segment
    cols_here = lax.axis_size("row") * segment
    ones_rows = jnp.ones((rows_here, 1, block_size), jnp.float32)
    ones_cols = jnp.ones((cols_here, 1, block_size), jnp.float32)
    degree_rows, degree_cols = local_terms(masked, row_index, col_index, ones_rows, ones_cols)
    degree = fold_terms(degree_rows, degree_cols)
    gains = strength[None, :, None]
    smoothed = jnp.zeros_like(raw_scores)
    residual = raw_scores
    direction = raw_scores
    norm_now = global_sum(total(residual * residual))
    for iteration in range(ITERS):
        panel_rows = lax.all_gather(direction, "col", axis=0, tiled=True)
        panel_cols = lax.all_gather(direction, "row", axis=0, tiled=True)
        row_part, col_part = local_terms(masked, row_index, col_index, panel_rows, panel_cols)
        product = fold_terms(row_part, col_part)
        image = direction + gains * (degree * direction - product)
        step_size = norm_now / global_sum(total(direction * image))
        smoothed = smoothed + step_size[None, :, None] * direction
        residual = residual - step_size[None, :, None] * image
        norm_next = global_sum(total(residual * residual))
        direction = residual + (norm_next / norm_now)[None, :, None] * direction
        norm_now = norm_next
    return (smoothed, residual)


def solution(mesh):
    placed = (
        P("row", "col", None, None, None),
        P("row", "col", None, None),
        P("row", "col"),
        P(),
        P(("row", "col"), None, None),
    )
    return jax.shard_map(
        shards,
        mesh=mesh,
        in_specs=placed,
        out_specs=(P(("row", "col"), None, None), P(("row", "col"), None, None)),
        check_vma=False,
    )
```

profile of v0, /device:TPU:1, one launch (start us, length us, event | category | flops | bytes accessed | tf_op | source)
XLA Modules:
  0.0 916.9 jit_solution(5695150841030016190)
XLA Ops:
  9.4 23.0 %all_gather.19 = f32[32,32,128]{2,1,0:T(8,128)S(1)} all-gather(f32[2,32,128]{2,1,0:T(8,128)} %param.13), channel_id=1, replica_groups=mesh['row'=16,'col'=16] {'col'}, dimensions={0}, use_global_device_ids=true | all-gather | bytes 557056 | tf_op jit(solution)/shard_map/all_gather | solution.py:55
  33.0 5.0 fusion.4
  38.1 4.9 scatter_fusion.1
  43.9 19.6 %all_gather.18 = f32[32,32,128]{2,1,0:T(8,128)S(1)} all-gather(f32[2,32,128]{2,1,0:T(8,128)S(1)} %copy-done.7), channel_id=1, replica_groups=mesh['row'=16,'col'=16] {'row'}, dimensions={0}, use_global_device_ids=true | all-gather | bytes 557056 | tf_op jit(solution)/shard_map/all_gather | solution.py:56
  64.9 6.2 fusion.5
  71.1 4.7 scatter_fusion
  88.7 58.4 %all-reduce.1 = f32[32,1,128]{2,0,1:T(8,128)S(1)} all-reduce(f32[32,1,128]{2,0,1:T(8,128)S(1)} %bitcast.49), channel_id=3, replica_groups=mesh['row'=16,'col'=16] {'row'}, use_global_device_ids=true, to_apply=%region_5.7.clone | all-reduce | flops 4096 | bytes 32768
  147.1 61.3 %all-reduce = f32[32,1,128]{2,0,1:T(8,128)S(1)} all-reduce(f32[32,1,128]{2,0,1:T(8,128)S(1)} %bitcast.48), channel_id=2, replica_groups=mesh['row'=16,'col'=16] {'col'}, use_global_device_ids=true, to_apply=%region_3.5.clone | all-reduce | flops 4096 | bytes 32768
  209.5 74.0 %all-reduce.2 = (f32[32]{0:T(128)S(1)}, f32[32]{0:T(128)S(1)}) all-reduce(f32[32]{0:T(128)S(1)} %get-tuple-element.5, f32[32]{0:T(128)S(1)} %get-tuple-element.4), channel_id=1, replica_groups=mesh['row'=16,'col'=16] {'row','col'}, use_global_device_ids=true, to_apply=%region_1.2 | all-reduce | flops 64 | bytes 512 | tf_op jit(solution)/shard_map/psum | solution.py:30
  284.5 74.5 %psum.44 = f32[32]{0:T(128)S(1)} all-reduce(f32[32]{0:T(128)S(1)} %get-tuple-element.10), channel_id=1, replica_groups=mesh['row'=16,'col'=16] {'row','col'}, use_global_device_ids=true, to_apply=%region_13.16 | all-reduce | flops 32 | bytes 256 | tf_op jit(solution)/shard_map/psum | solution.py:30
  359.0 17.2 %all_gather.21 = f32[32,32,128]{2,1,0:T(8,128)S(1)} all-gather(f32[2,32,128]{2,1,0:T(8,128)S(1)} %multiply_add_fusion.4), channel_id=1, replica_groups=mesh['row'=16,'col'=16] {'col'}, dimensions={0}, use_global_device_ids=true | all-gather | bytes 557056 | tf_op jit(solution)/shard_map/all_gather | solution.py:55
  387.7 19.2 %all_gather.20 = f32[32,32,128]{2,1,0:T(8,128)S(1)} all-gather(f32[2,32,128]{2,1,0:T(8,128)S(1)} %multiply_add_fusion.4), channel_id=1, replica_groups=mesh['row'=16,'col'=16] {'row'}, dimensions={0}, use_global_device_ids=true | all-gather | bytes 557056 | tf_op jit(solution)/shard_map/all_gather | solution.py:56
  408.3 6.2 fusion.3
  414.5 4.7 scatter_fusion.2
  420.1 38.4 %reduce-scatter.15.cloned.1.call-done = f32[2,32,128]{2,1,0:T(8,128)} async-done(((f32[32,32,128]{2,1,0:T(8,128)}), f32[2,32,128]{2,1,0:T(8,128)}) %reduce-scatter.15.cloned.1.call-update) | async-done | bytes 32784 | tf_op jit(solution)/shard_map/reduce_scatter | solution.py:20
  458.5 57.2 %reduce-scatter.13.cloned.1.call-done = f32[2,32,128]{2,1,0:T(8,128)} async-done(((f32[32,32,128]{2,1,0:T(8,128)}), f32[2,32,128]{2,1,0:T(8,128)}) %reduce-scatter.13.cloned.1.call-update) | async-done | bytes 32784 | tf_op jit(solution)/shard_map/reduce_scatter | solution.py:20
  516.7 79.6 %psum.45 = f32[32]{0:T(128)S(1)} all-reduce(f32[32]{0:T(128)S(1)} %multiply_reduce_fusion.2), channel_id=1, replica_groups=mesh['row'=16,'col'=16] {'row','col'}, use_global_device_ids=true, to_apply=%region_19.22 | all-reduce | flops 32 | bytes 256 | tf_op jit(solution)/shard_map/psum | solution.py:30
  597.2 72.4 %psum.46 = f32[32]{0:T(128)S(1)} all-reduce(f32[32]{0:T(128)S(1)} %get-tuple-element.8), channel_id=1, replica_groups=mesh['row'=16,'col'=16] {'row','col'}, use_global_device_ids=true, to_apply=%region_21.24 | all-reduce | flops 32 | bytes 256 | tf_op jit(solution)/shard_map/psum | solution.py:30
  669.6 18.1 %all_gather.23 = f32[32,32,128]{2,1,0:T(8,128)S(1)} all-gather(f32[2,32,128]{2,1,0:T(8,128)S(1)} %multiply_add_fusion.2), channel_id=1, replica_groups=mesh['row'=16,'col'=16] {'col'}, dimensions={0}, use_global_device_ids=true | all-gather | bytes 557056 | tf_op jit(solution)/shard_map/all_gather | solution.py:55
  699.1 19.2 %all_gather.22 = f32[32,32,128]{2,1,0:T(8,128)S(1)} all-gather(f32[2,32,128]{2,1,0:T(8,128)S(1)} %multiply_add_fusion.2), channel_id=1, replica_groups=mesh['row'=16,'col'=16] {'row'}, dimensions={0}, use_global_device_ids=true | all-gather | bytes 557056 | tf_op jit(solution)/shard_map/all_gather | solution.py:56
  719.8 5.3 fusion.1
  728.7 41.8 %reduce-scatter.19.cloned.1.call-done = f32[2,32,128]{2,1,0:T(8,128)} async-done(((f32[32,32,128]{2,1,0:T(8,128)}), f32[2,32,128]{2,1,0:T(8,128)}) %reduce-scatter.19.cloned.1.call-update) | async-done | bytes 32784 | tf_op jit(solution)/shard_map/reduce_scatter | solution.py:20
  770.5 57.3 %reduce-scatter.17.cloned.1.call-done = f32[2,32,128]{2,1,0:T(8,128)} async-done(((f32[32,32,128]{2,1,0:T(8,128)}), f32[2,32,128]{2,1,0:T(8,128)}) %reduce-scatter.17.cloned.1.call-update) | async-done | bytes 32784 | tf_op jit(solution)/shard_map/reduce_scatter | solution.py:20
  828.8 79.8 %psum.47 = f32[32]{0:T(128)S(1)} all-reduce(f32[32]{0:T(128)S(1)} %multiply_reduce_fusion), channel_id=1, replica_groups=mesh['row'=16,'col'=16] {'row','col'}, use_global_device_ids=true, to_apply=%region_27.30 | all-reduce | flops 32 | bytes 256 | tf_op jit(solution)/shard_map/psum | solution.py:30
  (82 shorter events, 52.6 us)
Async XLA Ops:
  7.2 201.3 %reduce-scatter.11.cloned.1.call-start = ((), (), s32[]{:S(2)}) async-start(), calls=%async_computation.7 | async-start | bytes 557056 | tf_op jit(solution)/shard_map/reduce_scatter | solution.py:20
  33.0 10.9 %copy-start.7 = (f32[2,32,128]{2,1,0:T(8,128)S(1)}, f32[2,32,128]{2,1,0:T(8,128)}, u32[]{:S(2)}) copy-start(f32[2,32,128]{2,1,0:T(8,128)} %param.13) | copy-start | bytes 98308
  38.0 26.9 %copy-start = (f32[1,1,40,128,128]{4,3,2,1,0:T(8,128)S(1)}, f32[1,1,40,128,128]{4,3,2,1,0:T(8,128)}, u32[]{:S(2)}) copy-start(f32[1,1,40,128,128]{4,3,2,1,0:T(8,128)} %param.9) | copy-start | bytes 7864324
  42.9 0.8 copy-start.3
  43.8 164.7 %reduce-scatter.9.cloned.1.call-start = ((), (), s32[]{:S(2)}) async-start(), calls=%async_computation.6 | async-start | bytes 557056 | tf_op jit(solution)/shard_map/reduce_scatter | solution.py:20
  71.1 6.8 copy-start.10
  71.1 7.4 copy-start.9
  75.8 0.8 copy-start.4
  76.7 381.8 %reduce-scatter.15.cloned.1.call-start = ((), (), s32[]{:S(2)}) async-start(), calls=%async_computation.9 | async-start | bytes 557056 | tf_op jit(solution)/shard_map/reduce_scatter | solution.py:20
  80.4 128.1 %copy-start.8 = (f32[32]{0:T(128)S(1)}, f32[32]{0:T(128)}, u32[]{:S(2)}) copy-start(f32[32]{0:T(128)} %param.12) | copy-start | bytes 388
  386.8 0.8 copy-start.5
  387.6 128.1 %reduce-scatter.13.cloned.1.call-start = ((), (), s32[]{:S(2)}) async-start(), calls=%async_computation.8 | async-start | bytes 557056 | tf_op jit(solution)/shard_map/reduce_scatter | solution.py:20
  419.2 0.8 copy-start.6
  420.0 350.5 %reduce-scatter.19.cloned.1.call-start = ((), (), s32[]{:S(2)}) async-start(), calls=%async_computation.11 | async-start | bytes 557056 | tf_op jit(solution)/shard_map/reduce_scatter | solution.py:20
  698.3 0.8 copy-start.2
  699.1 128.7 %reduce-scatter.17.cloned.1.call-start = ((), (), s32[]{:S(2)}) async-start(), calls=%async_computation.10 | async-start | bytes 557056 | tf_op jit(solution)/shard_map/reduce_scatter | solution.py:20
  727.9 0.8 copy-start.1
Sparse Core Ops, SparseCore 0:
  43.9 73.4 reduce-scatter.10
  120.0 55.2 reduce-scatter.8
  387.7 70.6 reduce-scatter.14
  461.0 54.6 reduce-scatter.12
  699.2 71.2 reduce-scatter.18
  773.0 54.7 reduce-scatter.16
where the time goes:
time: 918 us; the launch traced here: 917 us
  blocking collectives  616 us (67%)
  waiting for transfers between devices  195 us (21%)
  matrix products  37.9 us (4%)
  other arithmetic  35.4 us (4%)
  between operations  16.3 us (2%)
  local copies, waits for them, and re-layouts  15.9 us (2%)
    psum x5, blocking collectives, global_sum(): return lax.psum(partial_sum, ('row', 'col'))  380 us
    unnamed x2, blocking collectives  120 us
    reduce_scatter x3, waiting for transfers between devices, fold_terms(): lax.psum_scatter(row_part, 'col', scatter_dimension=0, tiled=True)  115 us
    reduce_scatter x3, waiting for transfers between devices, fold_terms(): lax.psum_scatter(col_part, 'row', scatter_dimension=0, tiled=True)  80.2 us
    all_gather x3, blocking collectives, shards(): panel_rows = lax.all_gather(direction, 'col', axis=0, tiled=True)  58.3 us
    all_gather x3, blocking collectives, shards(): panel_cols = lax.all_gather(direction, 'row', axis=0, tiled=True)  58 us
    dot_general x4, matrix products, local_terms(): jnp.einsum('crk,cik->cri', picked_cols, values, precision=lax.Precision.H...  22 us
  transfers between devices with their start and end apart: 6, of which 4 were waited for; matrix products, arithmetic and copies ran while one was open for 5% of the time, Pallas kernels for 0%

commit v1 on v0

--- a/solution.py
+++ b/solution.py
@@ -27,7 +27,7 @@
 
 
 def global_sum(partial_sum):
-    return lax.psum(partial_sum, ("row", "col"))
+    return lax.psum(lax.psum(partial_sum, "col"), "row")
 
 
 def shards(block_values, block_index, block_count, strength, raw_scores):

time: 918 us -> 848 us (0.924)
  blocking collectives: 616 us -> 540 us
    psum x5 -> x10, blocking collectives: 380 us -> 294 us  [global_sum(): return lax.psum(lax.psum(partial_sum, 'col'), 'row')]
    all_gather x3, blocking collectives: 58.3 us -> 70.5 us  [shards(): panel_rows = lax.all_gather(direction, 'col', axis=0, tiled=True)]
where the time goes in v1:
time: 848 us; the launch traced here: 842 us
  blocking collectives  540 us (64%)
  waiting for transfers between devices  197 us (23%)
  matrix products  37.9 us (4%)
  other arithmetic  35.4 us (4%)
  between operations  16.3 us (2%)
  local copies, waits for them, and re-layouts  15.9 us (2%)
    psum x10, blocking collectives, global_sum(): return lax.psum(lax.psum(partial_sum, 'col'), 'row')  294 us
    unnamed x2, blocking collectives  120 us
    reduce_scatter x3, waiting for transfers between devices, fold_terms(): lax.psum_scatter(row_part, 'col', scatter_dimension=0, tiled=True)  114 us
    reduce_scatter x3, waiting for transfers between devices, fold_terms(): lax.psum_scatter(col_part, 'row', scatter_dimension=0, tiled=True)  82.1 us
    all_gather x3, blocking collectives, shards(): panel_rows = lax.all_gather(direction, 'col', axis=0, tiled=True)  70.5 us
    all_gather x3, blocking collectives, shards(): panel_cols = lax.all_gather(direction, 'row', axis=0, tiled=True)  55.3 us
    dot_general x4, matrix products, local_terms(): jnp.einsum('crk,cik->cri', picked_cols, values, precision=lax.Precision.H...  22 us
  transfers between devices with their start and end apart: 6, of which 4 were waited for; matrix products, arithmetic and copies ran while one was open for 5% of the time, Pallas kernels for 0%

profile of v1, /device:TPU:1, one launch (start us, length us, event | category | flops | bytes accessed | tf_op | source)
XLA Modules:
  0.0 842.0 jit_solution(9813179164585319551)
XLA Ops:
  9.4 23.0 %all_gather.19 = f32[32,32,128]{2,1,0:T(8,128)S(1)} all-gather(f32[2,32,128]{2,1,0:T(8,128)} %param.13), channel_id=1, replica_groups=mesh['row'=16,'col'=16] {'col'}, dimensions={0}, use_global_device_ids=true | all-gather | bytes 557056 | tf_op jit(solution)/shard_map/all_gather | solution.py:55
  43.9 19.6 %all_gather.18 = f32[32,32,128]{2,1,0:T(8,128)S(1)} all-gather(f32[2,32,128]{2,1,0:T(8,128)S(1)} %copy-done.7), channel_id=1, replica_groups=mesh['row'=16,'col'=16] {'row'}, dimensions={0}, use_global_device_ids=true | all-gather | bytes 557056 | tf_op jit(solution)/shard_map/all_gather | solution.py:56
  64.9 6.2 fusion.5
  88.7 58.4 %all-reduce.1 = f32[32,1,128]{2,0,1:T(8,128)S(1)} all-reduce(f32[32,1,128]{2,0,1:T(8,128)S(1)} %bitcast.49), channel_id=3, replica_groups=mesh['row'=16,'col'=16] {'row'}, use_global_device_ids=true, to_apply=%region_6.8.clone | all-reduce | flops 4096 | bytes 32768
  147.1 61.3 %all-reduce = f32[32,1,128]{2,0,1:T(8,128)S(1)} all-reduce(f32[32,1,128]{2,0,1:T(8,128)S(1)} %bitcast.48), channel_id=2, replica_groups=mesh['row'=16,'col'=16] {'col'}, use_global_device_ids=true, to_apply=%region_4.6.clone | all-reduce | flops 4096 | bytes 32768
  209.5 26.4 %all-reduce.2 = (f32[32]{0:T(128)S(1)}, f32[32]{0:T(128)S(1)}) all-reduce(f32[32]{0:T(128)S(1)} %get-tuple-element.5, f32[32]{0:T(128)S(1)} %get-tuple-element.4), channel_id=1, replica_groups=mesh['row'=16,'col'=16] {'col'}, use_global_device_ids=true, to_apply=%region_1.2 | all-reduce | flops 64 | bytes 512 | tf_op jit(solution)/shard_map/psum | solution.py:30
  235.9 28.5 %all-reduce.3 = (f32[32]{0:T(128)S(1)}, f32[32]{0:T(128)S(1)}) all-reduce(f32[32]{0:T(128)S(1)} %get-tuple-element.6, f32[32]{0:T(128)S(1)} %get-tuple-element.7), channel_id=1, replica_groups=mesh['row'=16,'col'=16] {'row'}, use_global_device_ids=true, to_apply=%region_2.3 | all-reduce | flops 64 | bytes 512 | tf_op jit(solution)/shard_map/psum | solution.py:30
  265.4 30.5 %psum.88 = f32[32]{0:T(128)S(1)} all-reduce(f32[32]{0:T(128)S(1)} %get-tuple-element.12), channel_id=1, replica_groups=mesh['row'=16,'col'=16] {'col'}, use_global_device_ids=true, to_apply=%region_15.18 | all-reduce | flops 32 | bytes 256 | tf_op jit(solution)/shard_map/psum | solution.py:30
  295.9 30.2 %psum.89 = f32[32]{0:T(128)S(1)} all-reduce(f32[32]{0:T(128)S(1)} %psum.88), channel_id=1, replica_groups=mesh['row'=16,'col'=16] {'row'}, use_global_device_ids=true, to_apply=%region_16.19 | all-reduce | flops 32 | bytes 256 | tf_op jit(solution)/shard_map/psum | solution.py:30
  326.2 23.4 %all_gather.21 = f32[32,32,128]{2,1,0:T(8,128)S(1)} all-gather(f32[2,32,128]{2,1,0:T(8,128)S(1)} %multiply_add_fusion.4), channel_id=1, replica_groups=mesh['row'=16,'col'=16] {'col'}, dimensions={0}, use_global_device_ids=true | all-gather | bytes 557056 | tf_op jit(solution)/shard_map/all_gather | solution.py:55
  361.0 16.7 %all_gather.20 = f32[32,32,128]{2,1,0:T(8,128)S(1)} all-gather(f32[2,32,128]{2,1,0:T(8,128)S(1)} %multiply_add_fusion.4), channel_id=1, replica_groups=mesh['row'=16,'col'=16] {'row'}, dimensions={0}, use_global_device_ids=true | all-gather | bytes 557056 | tf_op jit(solution)/shard_map/all_gather | solution.py:56
  379.2 6.2 fusion.3
  391.0 38.7 %reduce-scatter.15.cloned.1.call-done = f32[2,32,128]{2,1,0:T(8,128)} async-done(((f32[32,32,128]{2,1,0:T(8,128)}), f32[2,32,128]{2,1,0:T(8,128)}) %reduce-scatter.15.cloned.1.call-update) | async-done | bytes 32784 | tf_op jit(solution)/shard_map/reduce_scatter | solution.py:20
  429.7 57.2 %reduce-scatter.13.cloned.1.call-done = f32[2,32,128]{2,1,0:T(8,128)} async-done(((f32[32,32,128]{2,1,0:T(8,128)}), f32[2,32,128]{2,1,0:T(8,128)}) %reduce-scatter.13.cloned.1.call-update) | async-done | bytes 32784 | tf_op jit(solution)/shard_map/reduce_scatter | solution.py:20
  487.9 26.4 %psum.90 = f32[32]{0:T(128)S(1)} all-reduce(f32[32]{0:T(128)S(1)} %multiply_reduce_fusion.2), channel_id=1, replica_groups=mesh['row'=16,'col'=16] {'col'}, use_global_device_ids=true, to_apply=%region_22.25 | all-reduce | flops 32 | bytes 256 | tf_op jit(solution)/shard_map/psum | solution.py:30
  514.3 33.1 %psum.91 = f32[32]{0:T(128)S(1)} all-reduce(f32[32]{0:T(128)S(1)} %psum.90), channel_id=1, replica_groups=mesh['row'=16,'col'=16] {'row'}, use_global_device_ids=true, to_apply=%region_23.26 | all-reduce | flops 32 | bytes 256 | tf_op jit(solution)/shard_map/psum | solution.py:30
  548.4 30.9 %psum.92 = f32[32]{0:T(128)S(1)} all-reduce(f32[32]{0:T(128)S(1)} %get-tuple-element.10), channel_id=1, replica_groups=mesh['row'=16,'col'=16] {'col'}, use_global_device_ids=true, to_apply=%region_25.28 | all-reduce | flops 32 | bytes 256 | tf_op jit(solution)/shard_map/psum | solution.py:30
  579.2 28.5 %psum.93 = f32[32]{0:T(128)S(1)} all-reduce(f32[32]{0:T(128)S(1)} %psum.92), channel_id=1, replica_groups=mesh['row'=16,'col'=16] {'row'}, use_global_device_ids=true, to_apply=%region_26.29 | all-reduce | flops 32 | bytes 256 | tf_op jit(solution)/shard_map/psum | solution.py:30
  607.8 24.0 %all_gather.23 = f32[32,32,128]{2,1,0:T(8,128)S(1)} all-gather(f32[2,32,128]{2,1,0:T(8,128)S(1)} %multiply_add_fusion.2), channel_id=1, replica_groups=mesh['row'=16,'col'=16] {'col'}, dimensions={0}, use_global_device_ids=true | all-gather | bytes 557056 | tf_op jit(solution)/shard_map/all_gather | solution.py:55
  643.2 19.1 %all_gather.22 = f32[32,32,128]{2,1,0:T(8,128)S(1)} all-gather(f32[2,32,128]{2,1,0:T(8,128)S(1)} %multiply_add_fusion.2), channel_id=1, replica_groups=mesh['row'=16,'col'=16] {'row'}, dimensions={0}, use_global_device_ids=true | all-gather | bytes 557056 | tf_op jit(solution)/shard_map/all_gather | solution.py:56
  672.6 43.4 %reduce-scatter.19.cloned.1.call-done = f32[2,32,128]{2,1,0:T(8,128)} async-done(((f32[32,32,128]{2,1,0:T(8,128)}), f32[2,32,128]{2,1,0:T(8,128)}) %reduce-scatter.19.cloned.1.call-update) | async-done | bytes 32784 | tf_op jit(solution)/shard_map/reduce_scatter | solution.py:20
  716.0 57.2 %reduce-scatter.17.cloned.1.call-done = f32[2,32,128]{2,1,0:T(8,128)} async-done(((f32[32,32,128]{2,1,0:T(8,128)}), f32[2,32,128]{2,1,0:T(8,128)}) %reduce-scatter.17.cloned.1.call-update) | async-done | bytes 32784 | tf_op jit(solution)/shard_map/reduce_scatter | solution.py:20
  774.2 26.4 %psum.94 = f32[32]{0:T(128)S(1)} all-reduce(f32[32]{0:T(128)S(1)} %multiply_reduce_fusion), channel_id=1, replica_groups=mesh['row'=16,'col'=16] {'col'}, use_global_device_ids=true, to_apply=%region_32.35 | all-reduce | flops 32 | bytes 256 | tf_op jit(solution)/shard_map/psum | solution.py:30
  800.6 33.1 %psum.95 = f32[32]{0:T(128)S(1)} all-reduce(f32[32]{0:T(128)S(1)} %psum.94), channel_id=1, replica_groups=mesh['row'=16,'col'=16] {'row'}, use_global_device_ids=true, to_apply=%region_33.36 | all-reduce | flops 32 | bytes 256 | tf_op jit(solution)/shard_map/psum | solution.py:30
  (87 shorter events, 77.2 us)
Async XLA Ops:
  7.2 201.3 %reduce-scatter.11.cloned.1.call-start = ((), (), s32[]{:S(2)}) async-start(), calls=%async_computation.7 | async-start | bytes 557056 | tf_op jit(solution)/shard_map/reduce_scatter | solution.py:20
  33.0 10.9 %copy-start.7 = (f32[2,32,128]{2,1,0:T(8,128)S(1)}, f32[2,32,128]{2,1,0:T(8,128)}, u32[]{:S(2)}) copy-start(f32[2,32,128]{2,1,0:T(8,128)} %param.13) | copy-start | bytes 98308
  38.0 26.9 %copy-start = (f32[1,1,40,128,128]{4,3,2,1,0:T(8,128)S(1)}, f32[1,1,40,128,128]{4,3,2,1,0:T(8,128)}, u32[]{:S(2)}) copy-start(f32[1,1,40,128,128]{4,3,2,1,0:T(8,128)} %param.9) | copy-start | bytes 7864324
  42.9 0.8 copy-start.3
  43.8 164.7 %reduce-scatter.9.cloned.1.call-start = ((), (), s32[]{:S(2)}) async-start(), calls=%async_computation.6 | async-start | bytes 557056 | tf_op jit(solution)/shard_map/reduce_scatter | solution.py:20
  71.1 6.8 copy-start.10
  71.1 7.4 copy-start.9
  75.8 0.8 copy-start.4
  76.7 353.0 %reduce-scatter.15.cloned.1.call-start = ((), (), s32[]{:S(2)}) async-start(), calls=%async_computation.9 | async-start | bytes 557056 | tf_op jit(solution)/shard_map/reduce_scatter | solution.py:20
  80.4 128.1 %copy-start.8 = (f32[32]{0:T(128)S(1)}, f32[32]{0:T(128)}, u32[]{:S(2)}) copy-start(f32[32]{0:T(128)} %param.12) | copy-start | bytes 388
  360.1 0.8 copy-start.5
  361.0 125.9 %reduce-scatter.13.cloned.1.call-start = ((), (), s32[]{:S(2)}) async-start(), calls=%async_computation.8 | async-start | bytes 557056 | tf_op jit(solution)/shard_map/reduce_scatter | solution.py:20
  390.1 0.8 copy-start.6
  390.9 325.0 %reduce-scatter.19.cloned.1.call-start = ((), (), s32[]{:S(2)}) async-start(), calls=%async_computation.11 | async-start | bytes 557056 | tf_op jit(solution)/shard_map/reduce_scatter | solution.py:20
  642.4 0.8 copy-start.2
  643.2 130.0 %reduce-scatter.17.cloned.1.call-start = ((), (), s32[]{:S(2)}) async-start(), calls=%async_computation.10 | async-start | bytes 557056 | tf_op jit(solution)/shard_map/reduce_scatter | solution.py:20
  671.8 0.8 copy-start.1
Sparse Core Ops, SparseCore 0:
  43.9 73.4 reduce-scatter.10
  120.0 55.2 reduce-scatter.8
  361.1 68.5 reduce-scatter.14
  432.2 54.6 reduce-scatter.12
  643.3 72.6 reduce-scatter.18
  718.5 54.6 reduce-scatter.16
